TPU v7x, 256 devices: a whole 4x4x8 slice. The times are simulated.
256 devices in a mesh: layer: 8 (over y, core), feat: 32 (over z, x).
Axes of the slice: x: 4, y: 4, z: 8, core: 2. Of those that a mesh axis runs over, the one named last changes fastest.
Arguments:
- top_grad: bfloat16 [256, 4608], P('feat'), may hold values from -6 to 6
- decoder: bfloat16 [8, 16384, 4608], P('layer', 'feat'), may hold values from -0.09375 to 0.09375
- encoder: bfloat16 [8, 16384, 4608], P('layer', 'feat'), may hold values from -0.03125 to 0.03125
- activations: bfloat16 [8, 256, 16384], P('layer', None, 'feat'), may hold values from 0.099609375 to 3
- block_ids: int32 [8, 32, 64], P('layer'), may hold values from 0 to 127, all different within a row
- block_counts: int32 [8, 32], P('layer'), may hold values from 1 to 64, 1024 in all within a row
Outputs:
- attribution: bfloat16 [8, 256, 16384], P('layer', None, 'feat')
- grads: float32 [8, 256, 4608], P('layer', 'feat')
Inputs may be any that keep to these rules, and one draw needn't show every extreme that they name: `block_ids`: within one row of the last dimension the ids are distinct; every block id appears somewhere. `block_counts`: for each layer the counts sum to 1024, and some tile of each layer has exactly 64.
All inputs are finite; a program needn't handle non-finite values.
Results may differ from a plain program's by a relative error of at most 0.024.
Values may be sent and summed in bfloat16 or wider, within the bound.
A program may use at most 64 MiB of HBM per device.

v0:
```python
import jax
import jax.numpy as jnp
from jax import lax
from jax.sharding import PartitionSpec as P

BLOCK = 128


def passed_along(value, axis, steps):
    count = lax.axis_size(axis)
    first, last = (max(0, -steps), min(count, count - steps))
    return lax.ppermute(value, axis, [(source, source + steps) for source in range(first, last)])


def body(top_grad, decoder, encoder, activations, block_ids, block_counts):
    layer_count = lax.axis_size("layer")
    tile_count = lax.axis_size("feat")
    section_index = lax.axis_index("layer")
    feat_index = lax.axis_index("feat")
    dec_rows = decoder[0]
    enc_rows = encoder[0]
    feat_dev = dec_rows.shape[0]
    model_width = dec_rows.shape[1]
    blk_dev = feat_dev // BLOCK
    tok_dev = top_grad.shape[0]
    list_width = block_ids.shape[2]
    listed = jnp.arange(list_width, dtype=jnp.int32)[None, :] < block_counts[0][:, None]
    owned = feat_index * blk_dev + jnp.arange(blk_dev, dtype=jnp.int32)
    matches = (block_ids[0][:, :, None] == owned[None, None, :]) & listed[:, :, None]
    tile_mask = jnp.any(matches, axis=1).astype(jnp.bfloat16)
    gated = (
        activations[0].reshape(tile_count, tok_dev, blk_dev, BLOCK) * tile_mask[:, None, :, None]
    )
    gated = gated.reshape(tile_count, tok_dev, feat_dev)
    group_count = 4
    group_rows = tok_dev // group_count
    step_total = group_count + layer_count - 1
    is_top = section_index == layer_count - 1

    def advance(step_count, carry):
        incoming, attr_buf, grad_buf = carry
        group_index = step_count - (layer_count - 1 - section_index)
        is_live = (group_index >= 0) & (group_index < group_count)
        group_slot = jnp.clip(group_index, 0, group_count - 1)
        row_offset = group_slot * group_rows
        top_rows = lax.dynamic_slice_in_dim(top_grad, row_offset, group_rows, 0).astype(jnp.float32)
        upstream = jnp.where(is_top, top_rows, incoming)
        gate_rows = lax.dynamic_slice_in_dim(gated, row_offset, group_rows, 1).reshape(
            tile_count * group_rows, feat_dev
        )
        scores = lax.dot_general(
            lax.all_gather(upstream.astype(jnp.bfloat16), "feat", axis=0, tiled=True),
            dec_rows,
            (((1,), (1,)), ((), ())),
            preferred_element_type=jnp.float32,
        )
        attributed = (scores * gate_rows).astype(jnp.bfloat16)
        summed = lax.psum_scatter(
            jnp.dot(attributed, enc_rows, preferred_element_type=jnp.float32).astype(jnp.bfloat16),
            "feat",
            scatter_dimension=0,
            tiled=True,
        ).astype(jnp.float32)
        updated = upstream + summed
        old_attr = lax.dynamic_slice_in_dim(attr_buf, row_offset, group_rows, 1)
        new_attr = jnp.where(
            is_live, attributed.reshape(tile_count, group_rows, feat_dev), old_attr
        )
        attr_buf = lax.dynamic_update_slice_in_dim(attr_buf, new_attr, row_offset, 1)
        old_grad = lax.dynamic_slice_in_dim(grad_buf, row_offset, group_rows, 0)
        new_grad = jnp.where(is_live, updated, old_grad)
        grad_buf = lax.dynamic_update_slice_in_dim(grad_buf, new_grad, row_offset, 0)
        passed = passed_along(updated.astype(jnp.bfloat16), "layer", -1).astype(updated.dtype)
        return (passed, attr_buf, grad_buf)

    start_state = (
        jnp.zeros((group_rows, model_width), jnp.float32),
        jnp.zeros((tile_count, tok_dev, feat_dev), jnp.bfloat16),
        jnp.zeros((tok_dev, model_width), jnp.float32),
    )
    final_state = lax.fori_loop(0, step_total, advance, start_state)
    attr_out = final_state[1].reshape(1, tile_count * tok_dev, feat_dev)
    grad_out = final_state[2][None]
    return (attr_out, grad_out)


def solution(mesh):
    placed = (
        P("feat", None),
        P("layer", "feat", None),
        P("layer", "feat", None),
        P("layer", None, "feat"),
        P("layer", None, None),
        P("layer", None),
    )
    return jax.shard_map(
        body,
        mesh=mesh,
        in_specs=placed,
        out_specs=(P("layer", None, "feat"), P("layer", "feat", None)),
        check_vma=False,
    )
```

profile of v0, /device:TPU:6, one launch (start us, length us, event | category | flops | bytes accessed | tf_op | source)
XLA Modules:
  0.0 2290.4 jit_solution(4350635033827040506)
XLA Ops:
  10.1 2273.0 %while.20 = (s32[]{:T(128)}, f32[2,4608]{1,0:T(2,128)S(1)}, bf16[32,8,512]{2,1,0:T(8,128)(2,1)S(1)}, f32[8,4608]{1,0:T(8,128)S(1)}, pred[]{:T(512)}, /*index=5*/...) while((s32[]{:T(128)}, f32[2,4608]{1,0:T(2,128)S(1)}, ...), condition=%wide.region_3.4_spmd.clone, body=%wide.region_1.3_spmd.clone.sunk | while | flops 604802048 | bytes 36239852 | solution.py:81
  11.1 52.2 %all-gather.3 = bf16[32,2,4608]{2,1,0:T(2,128)(2,1)S(1)} all-gather(bf16[1,2,4608]{2,1,0:T(2,128)(2,1)S(1)} %convert_bitcast_fusion.2), channel_id=1, replica_groups=mesh['layer'=8,'feat'=32] {'feat'}, dimensions={0}, use_global_device_ids=true | all-gather | bytes 608256 | tf_op jit(solution)/shard_map/while/body/eval_jaxpr/all_gather | solution.py:52
  63.8 4.0 fusion.17
  67.8 1.8 convolution_convert_fusion.2
  70.8 144.5 %all-reduce.5.cloned.1.call-done = bf16[64,4608]{1,0:T(8,128)(2,1)} async-done(((bf16[64,4608]{1,0:T(8,128)(2,1)}), bf16[64,4608]{1,0:T(8,128)(2,1)}) %all-reduce.5.cloned.1.call-update) | async-done | bytes 589840 | tf_op jit(solution)/shard_map/while
  216.3 1.3 collective-permute-start
  217.8 1.6 collective-permute-done
  220.4 48.6 %all-gather.3 = bf16[32,2,4608]{2,1,0:T(2,128)(2,1)S(1)} all-gather(bf16[1,2,4608]{2,1,0:T(2,128)(2,1)S(1)} %convert_bitcast_fusion.2), channel_id=1, replica_groups=mesh['layer'=8,'feat'=32] {'feat'}, dimensions={0}, use_global_device_ids=true | all-gather | bytes 608256 | tf_op jit(solution)/shard_map/while/body/eval_jaxpr/all_gather | solution.py:52
  269.4 4.0 fusion.17
  273.5 1.8 convolution_convert_fusion.2
  276.5 145.2 %all-reduce.5.cloned.1.call-done = bf16[64,4608]{1,0:T(8,128)(2,1)} async-done(((bf16[64,4608]{1,0:T(8,128)(2,1)}), bf16[64,4608]{1,0:T(8,128)(2,1)}) %all-reduce.5.cloned.1.call-update) | async-done | bytes 589840 | tf_op jit(solution)/shard_map/while
  424.1 1.6 collective-permute-done
  426.8 48.6 %all-gather.3 = bf16[32,2,4608]{2,1,0:T(2,128)(2,1)S(1)} all-gather(bf16[1,2,4608]{2,1,0:T(2,128)(2,1)S(1)} %convert_bitcast_fusion.2), channel_id=1, replica_groups=mesh['layer'=8,'feat'=32] {'feat'}, dimensions={0}, use_global_device_ids=true | all-gather | bytes 608256 | tf_op jit(solution)/shard_map/while/body/eval_jaxpr/all_gather | solution.py:52
  475.8 4.0 fusion.17
  479.8 1.8 convolution_convert_fusion.2
  482.9 145.2 %all-reduce.5.cloned.1.call-done = bf16[64,4608]{1,0:T(8,128)(2,1)} async-done(((bf16[64,4608]{1,0:T(8,128)(2,1)}), bf16[64,4608]{1,0:T(8,128)(2,1)}) %all-reduce.5.cloned.1.call-update) | async-done | bytes 589840 | tf_op jit(solution)/shard_map/while
  629.0 1.3 collective-permute-start
  630.5 1.6 collective-permute-done
  633.2 48.6 %all-gather.3 = bf16[32,2,4608]{2,1,0:T(2,128)(2,1)S(1)} all-gather(bf16[1,2,4608]{2,1,0:T(2,128)(2,1)S(1)} %convert_bitcast_fusion.2), channel_id=1, replica_groups=mesh['layer'=8,'feat'=32] {'feat'}, dimensions={0}, use_global_device_ids=true | all-gather | bytes 608256 | tf_op jit(solution)/shard_map/while/body/eval_jaxpr/all_gather | solution.py:52
  682.2 4.0 fusion.17
  686.2 1.8 convolution_convert_fusion.2
  689.3 145.2 %all-reduce.5.cloned.1.call-done = bf16[64,4608]{1,0:T(8,128)(2,1)} async-done(((bf16[64,4608]{1,0:T(8,128)(2,1)}), bf16[64,4608]{1,0:T(8,128)(2,1)}) %all-reduce.5.cloned.1.call-update) | async-done | bytes 589840 | tf_op jit(solution)/shard_map/while
  835.4 1.3 collective-permute-start
  836.9 1.6 collective-permute-done
  839.5 48.6 %all-gather.3 = bf16[32,2,4608]{2,1,0:T(2,128)(2,1)S(1)} all-gather(bf16[1,2,4608]{2,1,0:T(2,128)(2,1)S(1)} %convert_bitcast_fusion.2), channel_id=1, replica_groups=mesh['layer'=8,'feat'=32] {'feat'}, dimensions={0}, use_global_device_ids=true | all-gather | bytes 608256 | tf_op jit(solution)/shard_map/while/body/eval_jaxpr/all_gather | solution.py:52
  888.6 4.0 fusion.17
  892.6 1.8 convolution_convert_fusion.2
  895.6 145.2 %all-reduce.5.cloned.1.call-done = bf16[64,4608]{1,0:T(8,128)(2,1)} async-done(((bf16[64,4608]{1,0:T(8,128)(2,1)}), bf16[64,4608]{1,0:T(8,128)(2,1)}) %all-reduce.5.cloned.1.call-update) | async-done | bytes 589840 | tf_op jit(solution)/shard_map/while
  1041.8 1.3 collective-permute-start
  1043.3 1.6 collective-permute-done
  1045.9 48.6 %all-gather.3 = bf16[32,2,4608]{2,1,0:T(2,128)(2,1)S(1)} all-gather(bf16[1,2,4608]{2,1,0:T(2,128)(2,1)S(1)} %convert_bitcast_fusion.2), channel_id=1, replica_groups=mesh['layer'=8,'feat'=32] {'feat'}, dimensions={0}, use_global_device_ids=true | all-gather | bytes 608256 | tf_op jit(solution)/shard_map/while/body/eval_jaxpr/all_gather | solution.py:52
  1094.9 4.0 fusion.17
  1099.0 1.8 convolution_convert_fusion.2
  1102.0 145.2 %all-reduce.5.cloned.1.call-done = bf16[64,4608]{1,0:T(8,128)(2,1)} async-done(((bf16[64,4608]{1,0:T(8,128)(2,1)}), bf16[64,4608]{1,0:T(8,128)(2,1)}) %all-reduce.5.cloned.1.call-update) | async-done | bytes 589840 | tf_op jit(solution)/shard_map/while
  1249.6 1.6 collective-permute-done
  1252.3 48.6 %all-gather.3 = bf16[32,2,4608]{2,1,0:T(2,128)(2,1)S(1)} all-gather(bf16[1,2,4608]{2,1,0:T(2,128)(2,1)S(1)} %convert_bitcast_fusion.2), channel_id=1, replica_groups=mesh['layer'=8,'feat'=32] {'feat'}, dimensions={0}, use_global_device_ids=true | all-gather | bytes 608256 | tf_op jit(solution)/shard_map/while/body/eval_jaxpr/all_gather | solution.py:52
  1301.3 4.0 fusion.17
  1305.3 1.8 convolution_convert_fusion.2
  1308.4 145.2 %all-reduce.5.cloned.1.call-done = bf16[64,4608]{1,0:T(8,128)(2,1)} async-done(((bf16[64,4608]{1,0:T(8,128)(2,1)}), bf16[64,4608]{1,0:T(8,128)(2,1)}) %all-reduce.5.cloned.1.call-update) | async-done | bytes 589840 | tf_op jit(solution)/shard_map/while
  1456.0 1.6 collective-permute-done
  1458.6 48.6 %all-gather.3 = bf16[32,2,4608]{2,1,0:T(2,128)(2,1)S(1)} all-gather(bf16[1,2,4608]{2,1,0:T(2,128)(2,1)S(1)} %convert_bitcast_fusion.2), channel_id=1, replica_groups=mesh['layer'=8,'feat'=32] {'feat'}, dimensions={0}, use_global_device_ids=true | all-gather | bytes 608256 | tf_op jit(solution)/shard_map/while/body/eval_jaxpr/all_gather | solution.py:52
  1507.7 4.0 fusion.17
  1511.7 1.8 convolution_convert_fusion.2
  1514.8 145.2 %all-reduce.5.cloned.1.call-done = bf16[64,4608]{1,0:T(8,128)(2,1)} async-done(((bf16[64,4608]{1,0:T(8,128)(2,1)}), bf16[64,4608]{1,0:T(8,128)(2,1)}) %all-reduce.5.cloned.1.call-update) | async-done | bytes 589840 | tf_op jit(solution)/shard_map/while
  1660.9 1.3 collective-permute-start
  1662.4 1.6 collective-permute-done
  1665.0 48.6 %all-gather.3 = bf16[32,2,4608]{2,1,0:T(2,128)(2,1)S(1)} all-gather(bf16[1,2,4608]{2,1,0:T(2,128)(2,1)S(1)} %convert_bitcast_fusion.2), channel_id=1, replica_groups=mesh['layer'=8,'feat'=32] {'feat'}, dimensions={0}, use_global_device_ids=true | all-gather | bytes 608256 | tf_op jit(solution)/shard_map/while/body/eval_jaxpr/all_gather | solution.py:52
  1714.1 4.0 fusion.17
  1718.1 1.8 convolution_convert_fusion.2
  1721.1 145.2 %all-reduce.5.cloned.1.call-done = bf16[64,4608]{1,0:T(8,128)(2,1)} async-done(((bf16[64,4608]{1,0:T(8,128)(2,1)}), bf16[64,4608]{1,0:T(8,128)(2,1)}) %all-reduce.5.cloned.1.call-update) | async-done | bytes 589840 | tf_op jit(solution)/shard_map/while
  1867.3 1.3 collective-permute-start
  1868.8 1.6 collective-permute-done
  1871.4 48.6 %all-gather.3 = bf16[32,2,4608]{2,1,0:T(2,128)(2,1)S(1)} all-gather(bf16[1,2,4608]{2,1,0:T(2,128)(2,1)S(1)} %convert_bitcast_fusion.2), channel_id=1, replica_groups=mesh['layer'=8,'feat'=32] {'feat'}, dimensions={0}, use_global_device_ids=true | all-gather | bytes 608256 | tf_op jit(solution)/shard_map/while/body/eval_jaxpr/all_gather | solution.py:52
  1920.4 4.0 fusion.17
  1924.5 1.8 convolution_convert_fusion.2
  1927.5 145.2 %all-reduce.5.cloned.1.call-done = bf16[64,4608]{1,0:T(8,128)(2,1)} async-done(((bf16[64,4608]{1,0:T(8,128)(2,1)}), bf16[64,4608]{1,0:T(8,128)(2,1)}) %all-reduce.5.cloned.1.call-update) | async-done | bytes 589840 | tf_op jit(solution)/shard_map/while
  2073.7 1.3 collective-permute-start
  2075.1 1.6 collective-permute-done
  2077.8 48.6 %all-gather.3 = bf16[32,2,4608]{2,1,0:T(2,128)(2,1)S(1)} all-gather(bf16[1,2,4608]{2,1,0:T(2,128)(2,1)S(1)} %convert_bitcast_fusion.2), channel_id=1, replica_groups=mesh['layer'=8,'feat'=32] {'feat'}, dimensions={0}, use_global_device_ids=true | all-gather | bytes 608256 | tf_op jit(solution)/shard_map/while/body/eval_jaxpr/all_gather | solution.py:52
  2126.8 4.0 fusion.17
  2130.8 1.8 convolution_convert_fusion.2
  2133.9 145.2 %all-reduce.5.cloned.1.call-done = bf16[64,4608]{1,0:T(8,128)(2,1)} async-done(((bf16[64,4608]{1,0:T(8,128)(2,1)}), bf16[64,4608]{1,0:T(8,128)(2,1)}) %all-reduce.5.cloned.1.call-update) | async-done | bytes 589840 | tf_op jit(solution)/shard_map/while
  2280.0 1.3 collective-permute-start
  2281.5 1.6 collective-permute-done
  (183 shorter events, 42.2 us)
Async XLA Ops:
  10.2 205.1 %all-reduce.5.cloned.1.call-start = ((), (), s32[]{:S(2)}) async-start(), calls=%async_computation | async-start | bytes 1179648 | tf_op jit(solution)/shard_map/while
  63.7 4.0 copy-start
  63.7 5.9 copy-start.3
  216.3 3.1 collective-permute-start
  219.4 202.3 %all-reduce.5.cloned.1.call-start = ((), (), s32[]{:S(2)}) async-start(), calls=%async_computation | async-start | bytes 1179648 | tf_op jit(solution)/shard_map/while
  269.4 4.0 copy-start
  269.4 5.9 copy-start.3
  422.7 3.1 collective-permute-start
  425.8 202.3 %all-reduce.5.cloned.1.call-start = ((), (), s32[]{:S(2)}) async-start(), calls=%async_computation | async-start | bytes 1179648 | tf_op jit(solution)/shard_map/while
  475.8 4.1 copy-start
  475.8 5.9 copy-start.3
  629.0 3.1 collective-permute-start
  632.2 202.3 %all-reduce.5.cloned.1.call-start = ((), (), s32[]{:S(2)}) async-start(), calls=%async_computation | async-start | bytes 1179648 | tf_op jit(solution)/shard_map/while
  682.2 4.0 copy-start
  682.2 5.9 copy-start.3
  835.4 3.1 collective-permute-start
  838.5 202.3 %all-reduce.5.cloned.1.call-start = ((), (), s32[]{:S(2)}) async-start(), calls=%async_computation | async-start | bytes 1179648 | tf_op jit(solution)/shard_map/while
  888.5 4.0 copy-start
  888.6 5.9 copy-start.3
  1041.8 3.1 collective-permute-start
  1044.9 202.3 %all-reduce.5.cloned.1.call-start = ((), (), s32[]{:S(2)}) async-start(), calls=%async_computation | async-start | bytes 1179648 | tf_op jit(solution)/shard_map/while
  1094.9 4.0 copy-start
  1094.9 5.9 copy-start.3
  1248.2 3.1 collective-permute-start
  1251.3 202.3 %all-reduce.5.cloned.1.call-start = ((), (), s32[]{:S(2)}) async-start(), calls=%async_computation | async-start | bytes 1179648 | tf_op jit(solution)/shard_map/while
  1301.3 4.0 copy-start
  1301.3 5.9 copy-start.3
  1454.5 3.1 collective-permute-start
  1457.7 202.3 %all-reduce.5.cloned.1.call-start = ((), (), s32[]{:S(2)}) async-start(), calls=%async_computation | async-start | bytes 1179648 | tf_op jit(solution)/shard_map/while
  1507.7 4.0 copy-start
  1507.7 5.9 copy-start.3
  1660.9 3.1 collective-permute-start
  1664.0 202.3 %all-reduce.5.cloned.1.call-start = ((), (), s32[]{:S(2)}) async-start(), calls=%async_computation | async-start | bytes 1179648 | tf_op jit(solution)/shard_map/while
  1714.0 4.0 copy-start
  1714.1 5.9 copy-start.3
  1867.3 3.1 collective-permute-start
  1870.4 202.3 %all-reduce.5.cloned.1.call-start = ((), (), s32[]{:S(2)}) async-start(), calls=%async_computation | async-start | bytes 1179648 | tf_op jit(solution)/shard_map/while
  1920.4 4.0 copy-start
  1920.4 5.9 copy-start.3
  2073.7 3.1 collective-permute-start
  2076.8 202.3 %all-reduce.5.cloned.1.call-start = ((), (), s32[]{:S(2)}) async-start(), calls=%async_computation | async-start | bytes 1179648 | tf_op jit(solution)/shard_map/while
  2126.8 4.0 copy-start
  2126.8 5.9 copy-start.3
  2280.0 3.1 collective-permute-start
  2283.2 0.7 copy-start.1
  2283.2 0.7 copy-start.2
Sparse Core Ops, SparseCore 0:
  69.7 145.5 all-reduce.4
  275.4 146.2 all-reduce.4
  481.8 146.2 all-reduce.4
  688.1 146.2 all-reduce.4
  894.5 146.2 all-reduce.4
  1100.9 146.2 all-reduce.4
  1307.3 146.2 all-reduce.4
  1513.6 146.2 all-reduce.4
  1720.0 146.2 all-reduce.4
  1926.4 146.2 all-reduce.4
  2132.8 146.2 all-reduce.4
where the time goes:
time: 2300 us; the launch traced here: 2290 us
  waiting for transfers between devices  1610 us (70%)
  blocking collectives  538 us (23%)
  matrix products  63.8 us (3%)
  other arithmetic  26.4 us (1%)
    while x22, waiting for transfers between devices  1600 us
    all_gather x11, blocking collectives, advance(): lax.all_gather(upstream.astype(jnp.bfloat16), 'feat', axis=0, tiled=True)  538 us
  transfers between devices with their start and end apart: 22, of which 22 were waited for; matrix products, arithmetic and copies ran while one was open for 0% of the time, Pallas kernels for 0%

commit v1 on v0

v1 whole, which is shorter than its diff:
```python
import functools

import jax
import jax.numpy as jnp
from jax import lax
from jax.experimental import pallas as pl
from jax.experimental.pallas import tpu as pltpu
from jax.sharding import PartitionSpec as P

BLOCK = 128
MESH = pl.DeviceIdType.MESH
NX = 4


def kernel(
    layers, nz, nx, top_ref, dec_hbm, enc_hbm, act_hbm, ids_ref, cnt_ref, attr_out, grad_out,
    dec_v, enc_v, act_v, gate_v, attr_v, hsend, hout, gin, gnew, agbuf, pbuf, pown, rsx, zsend, rsz, coll,
    load_sem, attr_sem, top_send, top_recv, agz_send, agz_recv, agx_send, agx_recv, rsx_send, rsx_recv,
    rsz_send, rsz_recv, gin_send, gin_recv, coll_send, coll_recv,
):
    feats, width = dec_v.shape[1], dec_v.shape[2]
    tok = top_ref.shape[0]
    rows = nz * tok
    groups = nx
    layer = lax.axis_index("layer")
    feat = lax.axis_index("feat")
    z = feat // nx
    x = feat % nx
    lower = (layer + layers - 1) % layers
    upper = (layer + 1) % layers
    is_top = layer == layers - 1

    def z_peer(d):
        return ((z + d) % nz) * nx + x

    def x_peer(d):
        return z * nx + (x + d) % nx

    def cols(j):
        return pl.ds(pl.multiple_of(j * width, 128), width)

    def remote(src, dst, send, recv, where, peer):
        return pltpu.make_async_remote_copy(
            src_ref=src, dst_ref=dst, send_sem=send, recv_sem=recv, device_id=(where, peer), device_id_type=MESH
        )

    def settle(ref, sem):
        pltpu.make_async_copy(ref, ref, sem).wait()

    loads = [pltpu.make_async_copy(act_hbm.at[:, j], act_v.at[j], load_sem.at[2 * nx + j]) for j in range(nx)]
    loads += [pltpu.make_async_copy(dec_hbm.at[:, cols(j)], dec_v.at[j], load_sem.at[j]) for j in range(nx)]
    loads += [pltpu.make_async_copy(enc_hbm.at[:, cols(j)], enc_v.at[j], load_sem.at[nx + j]) for j in range(nx)]
    for load in loads:
        load.start()

    barrier = pltpu.get_barrier_semaphore()
    for d in range(1, nx):
        pl.semaphore_signal(barrier, inc=1, device_id=(layer, x_peer(d)), device_id_type=MESH)
    for d in range(1, nz):
        pl.semaphore_signal(barrier, inc=1, device_id=(layer, z_peer(d)), device_id_type=MESH)
    for d in range(nz):
        pl.semaphore_signal(barrier, inc=1, device_id=(lower, z_peer(d)), device_id_type=MESH)
        pl.semaphore_signal(barrier, inc=1, device_id=(upper, z_peer(d)), device_id_type=MESH)
    pl.semaphore_wait(barrier, nx - 1 + nz - 1 + 2 * nz)

    far_z = sorted(range(1, nz), key=lambda d: -min(d, nz - d))
    far_x = sorted(range(1, nx), key=lambda d: -min(d, nx - d))
    near_x = far_x[::-1]

    @pl.when(is_top)
    def _():
        pltpu.make_async_copy(top_ref.at[:, cols(x)], hsend.at[x], top_recv).start()
        for d in far_x:
            remote(
                top_ref.at[:, cols((x + d) % nx)], hsend.at[x], top_send, top_recv, layer, x_peer(d)
            ).start()
        settle(hsend, top_recv)

        @pl.loop(0, groups)
        def _(g):
            for d in far_z:
                remote(hsend.at[g], agbuf.at[g, x, z], agz_send, agz_recv.at[g], layer, z_peer(d)).start()
            pltpu.make_async_copy(hsend.at[g], agbuf.at[g, x, z], agz_recv.at[g]).start()
            gin[g] = hsend[g].astype(jnp.float32)

    tiles = nz * nx
    listed_ids = ids_ref[...]
    width_ids = listed_ids.shape[1]
    eye = lax.broadcasted_iota(jnp.int32, (tiles, tiles), 0) == lax.broadcasted_iota(jnp.int32, (tiles, tiles), 1)
    counts = jnp.sum(jnp.where(eye, jnp.broadcast_to(cnt_ref[...], (tiles, tiles)), 0), axis=1, keepdims=True)
    listed = lax.broadcasted_iota(jnp.int32, (tiles, width_ids), 1) < counts
    blk_dev = feats // BLOCK
    parts = []
    for b in range(blk_dev):
        hit = jnp.where(listed & (listed_ids == feat * blk_dev + b), 1.0, 0.0)
        parts.append(jnp.broadcast_to(jnp.max(hit, axis=1, keepdims=True), (tiles, BLOCK)))
    tile_mask = jnp.concatenate(parts, axis=1).astype(jnp.bfloat16)
    for j in range(nx):
        loads[j].wait()
    row_tile = (lax.broadcasted_iota(jnp.int32, (rows, tiles), 0) // tok) * nx
    col_tile = lax.broadcasted_iota(jnp.int32, (rows, tiles), 1)
    for j in range(groups):
        pick = jnp.where(row_tile + j == col_tile, 1.0, 0.0).astype(jnp.bfloat16)
        mask = jnp.dot(pick, tile_mask, preferred_element_type=jnp.float32)
        gate_v[j] = act_v[j].astype(jnp.float32).reshape(rows, feats) * mask
    for load in loads[nx:]:
        load.wait()

    def forward(g):
        settle(agbuf.at[g, x], agz_recv.at[g])
        for d in far_x:
            remote(
                agbuf.at[g, x], agbuf.at[g, x], agx_send, agx_recv.at[g, d - 1], layer, x_peer(d)
            ).start()

    def scores_of(g, j):
        h = agbuf[g, j].reshape(rows, width)
        return lax.dot_general(h, dec_v[j], (((1,), (1,)), ((), ())), preferred_element_type=jnp.float32)

    def attribute(g):
        total = scores_of(g, x)
        for d in near_x:
            j = (x + nx - d) % nx
            settle(agbuf.at[g, j], agx_recv.at[g, d - 1])
            total = total + scores_of(g, j)
        attr = total * gate_v[g]
        attr_v[g] = attr.reshape(nz, tok, feats).astype(jnp.bfloat16)
        attr = attr.astype(jnp.bfloat16)
        pltpu.make_async_copy(attr_v.at[g], attr_out.at[:, g], attr_sem).start()
        for d in far_x:
            j = (x + d) % nx
            part = jnp.dot(attr, enc_v[j], preferred_element_type=jnp.float32)
            pbuf[g, d - 1] = part.astype(jnp.bfloat16)
            remote(
                pbuf.at[g, d - 1], rsx.at[g, d - 1], rsx_send, rsx_recv.at[g, d - 1], layer, x_peer(d)
            ).start()
        pown[g] = jnp.dot(attr, enc_v[x], preferred_element_type=jnp.float32)

    def reduce_x(g):
        total = pown[g]
        for d in near_x:
            settle(rsx.at[g, d - 1], rsx_recv.at[g, d - 1])
            total = total + rsx[g, d - 1].astype(jnp.float32)
        zsend[g] = total.reshape(nz, tok, width).astype(jnp.bfloat16)
        for d in far_z:
            remote(
                zsend.at[g, (z + d) % nz], rsz.at[g, d - 1], rsz_send, rsz_recv.at[g], layer, z_peer(d)
            ).start()

    def reduce_z(g):
        @pl.when(jnp.logical_not(is_top))
        def _():
            settle(gin.at[g], gin_recv.at[g])

        settle(rsz.at[g], rsz_recv.at[g])
        total = zsend[g, z].astype(jnp.float32)
        for d in range(1, nz):
            total = total + rsz[g, d - 1].astype(jnp.float32)
        total = total + gin[g]
        gnew[g] = total
        hout[g] = total.astype(jnp.bfloat16)

        @pl.when(layer > 0)
        def _():
            for d in far_z + [0]:
                remote(hout.at[g], agbuf.at[g, x, z], agz_send, agz_recv.at[g], lower, z_peer(d)).start()
            remote(gnew.at[g], gin.at[g], gin_send, gin_recv.at[g], lower, feat).start()

        @pl.when(x != g)
        def _():
            remote(gnew.at[g], coll.at[x], coll_send, coll_recv, layer, z * nx + g).start()

        @pl.when(x == g)
        def _():
            pltpu.make_async_copy(gnew.at[g], coll.at[x], coll_recv).start()

    @pl.loop(0, groups + 1)
    def _(step):
        @pl.when(step < groups)
        def _():
            forward(step)

        @pl.when(step > 0)
        def _():
            reduce_x(step - 1)

        @pl.when(step < groups)
        def _():
            attribute(step)

        @pl.when(step > 0)
        def _():
            reduce_z(step - 1)

    settle(coll, coll_recv)
    for j in range(nx):
        grad_out[:, j * width:(j + 1) * width] = coll[j]

    settle(attr_v, attr_sem)
    settle(agbuf.at[:, pl.ds(0, nx - 1)], agx_send)
    settle(pbuf, rsx_send)
    settle(zsend.at[:, pl.ds(0, nz - 1)], rsz_send)
    settle(coll.at[pl.ds(0, nx - 1)], coll_send)

    @pl.when(is_top)
    def _():
        settle(hsend.at[pl.ds(0, nx - 1)], top_send)
        settle(zsend.at[:, pl.ds(0, nz - 1)], agz_send)

    @pl.when(layer > 0)
    def _():
        settle(zsend, agz_send)
        settle(gnew, gin_send)


def body(nx, top_grad, decoder, encoder, activations, block_ids, block_counts):
    layers = lax.axis_size("layer")
    tiles = lax.axis_size("feat")
    nz = tiles // nx
    dec, enc = decoder[0], encoder[0]
    feats, model = dec.shape
    width = model // nx
    tok = top_grad.shape[0]
    rows = nz * tok
    act = activations[0].reshape(nz, nx, tok, feats)
    bf16, f32 = jnp.bfloat16, jnp.float32
    dma = pltpu.SemaphoreType.DMA
    vmem = pl.BlockSpec(memory_space=pltpu.VMEM)
    hbm = pl.BlockSpec(memory_space=pl.ANY)
    attr, grads = pl.pallas_call(
        functools.partial(kernel, layers, nz, nx),
        out_shape=(
            jax.ShapeDtypeStruct((nz, nx, tok, feats), bf16),
            jax.ShapeDtypeStruct((tok, model), f32),
        ),
        in_specs=[vmem, hbm, hbm, hbm, vmem, vmem],
        out_specs=(hbm, vmem),
        scratch_shapes=[
            pltpu.VMEM((nx, feats, width), bf16),
            pltpu.VMEM((nx, feats, width), bf16),
            pltpu.VMEM((nx, nz, tok, feats), bf16),
            pltpu.VMEM((nx, rows, feats), f32),
            pltpu.VMEM((nx, nz, tok, feats), bf16),
            pltpu.VMEM((nx, tok, width), bf16),
            pltpu.VMEM((nx, tok, width), bf16),
            pltpu.VMEM((nx, tok, width), f32),
            pltpu.VMEM((nx, tok, width), f32),
            pltpu.VMEM((nx, nx, nz, tok, width), bf16),
            pltpu.VMEM((nx, nx - 1, rows, width), bf16),
            pltpu.VMEM((nx, rows, width), f32),
            pltpu.VMEM((nx, nx - 1, rows, width), bf16),
            pltpu.VMEM((nx, nz, tok, width), bf16),
            pltpu.VMEM((nx, nz - 1, tok, width), bf16),
            pltpu.VMEM((nx, tok, width), f32),
            dma((3 * nx,)),
            dma,
            dma,
            dma,
            dma,
            dma((nx,)),
            dma,
            dma((nx, nx - 1)),
            dma,
            dma((nx, nx - 1)),
            dma,
            dma((nx,)),
            dma,
            dma((nx,)),
            dma,
            dma,
        ],
        compiler_params=pltpu.CompilerParams(
            collective_id=0, has_side_effects=True, vmem_limit_bytes=60 * 1024 * 1024
        ),
    )(top_grad, dec, enc, act, block_ids[0], block_counts)
    return (attr.reshape(1, tiles * tok, feats), grads[None])


def solution(mesh, nx=NX):
    placed = (
        P("feat", None),
        P("layer", "feat", None),
        P("layer", "feat", None),
        P("layer", None, "feat"),
        P("layer", None, None),
        P("layer", None),
    )
    return jax.shard_map(
        functools.partial(body, nx),
        mesh=mesh,
        in_specs=placed,
        out_specs=(P("layer", None, "feat"), P("layer", "feat", None)),
        check_vma=False,
    )
```

time: 2300 us -> 283 us (0.12)
  waiting for transfers between devices: 1610 us -> 0 us
  blocking collectives: 538 us -> 0 us
  Pallas kernels: 0 us -> 279 us
  matrix products: 63.8 us -> 0 us
  other arithmetic: 26.4 us -> 0 us
    while x22 -> x0, waiting for transfers between devices: 1600 us -> none
    all_gather x11 -> x0, blocking collectives: 538 us -> none  [advance(): lax.all_gather(upstream.astype(jnp.bfloat16), 'feat', axis=0, tiled=True)]
    pallas_call x0 -> x1, Pallas kernels: none -> 279 us  [body(): pl.pallas_call(functools.partial(kernel, layers, nz, nx), out_shape=(jax....]
    dot_general x22 -> x0, matrix products: 63.8 us -> none  [the longest x11 44.2 us: advance(): lax.dot_general(lax.all_gather(upstream.astype(jnp.bfloat16), 'feat', axi...]
  transfers between devices with their start and end apart: 22 -> 0, of which waited for: 22 -> 0; matrix products, arithmetic and copies ran while one was open for 0% -> 0% of each run, Pallas kernels for 0% -> 0%
where the time goes in v1:
time: 283 us
  Pallas kernels  279 us (99%)
  local copies, waits for them, and re-layouts  3.25 us (1%)
    pallas_call x1, Pallas kernels, body(): pl.pallas_call(functools.partial(kernel, layers, nz, nx), out_shape=(jax....  279 us

profile of v1, /device:TPU:6, one launch (start us, length us, event | category | flops | bytes accessed | tf_op | source)
XLA Modules:
  0.0 283.2 jit_solution(12655333721154906596)
XLA Ops:
  0.6 279.4 %shard_map.77 = (bf16[8,4,8,512]{3,2,1,0:T(8,128)(2,1)}, f32[8,4608]{1,0:T(8,128)}) custom-call(bf16[8,4608]{1,0:T(8,128)(2,1)} %top_ref.1, bf16[512,4608]{1,0:T(8,128)(2,1)} %bitcast.6, bf16[512,4608]{1,0:T(8,128)(2,1)} %bitcast.7, bf16[8,4,8,512]{3,2,1,0:T(8,128)(2,1)} %bitcast.8, s32[32,64]{1,0:T(8,128)} %bitcast.11, s32[1,32]{1,0:T(1,128)} %cnt_ref.1), custom_call_target="tpu_custom_call" | custom-call | tf_op jit(solution)/shard_map/pallas_call | solution.py:230
  280.0 1.7 copy.10
  281.7 1.6 copy.11

commit v2 on v1

--- a/solution.py
+++ b/solution.py
@@ -79,8 +79,8 @@
         @pl.loop(0, groups)
         def _(g):
             for d in far_z:
-                remote(hsend.at[g], agbuf.at[g, x, z], agz_send, agz_recv.at[g], layer, z_peer(d)).start()
-            pltpu.make_async_copy(hsend.at[g], agbuf.at[g, x, z], agz_recv.at[g]).start()
+                remote(hsend.at[g], agbuf.at[g, x, z], agz_send, agz_recv.at[g, d], layer, z_peer(d)).start()
+            pltpu.make_async_copy(hsend.at[g], agbuf.at[g, x, z], agz_recv.at[g, 0]).start()
             gin[g] = hsend[g].astype(jnp.float32)
 
     tiles = nz * nx
@@ -107,11 +107,13 @@
         load.wait()
 
     def forward(g):
-        settle(agbuf.at[g, x], agz_recv.at[g])
-        for d in far_x:
-            remote(
-                agbuf.at[g, x], agbuf.at[g, x], agx_send, agx_recv.at[g, d - 1], layer, x_peer(d)
-            ).start()
+        for d in [0] + far_z[::-1]:
+            k = (z + nz - d) % nz
+            settle(agbuf.at[g, x, k], agz_recv.at[g, d])
+            for e in far_x:
+                remote(
+                    agbuf.at[g, x, k], agbuf.at[g, x, k], agx_send, agx_recv.at[g, e - 1], layer, x_peer(e)
+                ).start()
 
     def scores_of(g, j):
         h = agbuf[g, j].reshape(rows, width)
@@ -128,24 +130,27 @@
         attr = attr.astype(jnp.bfloat16)
         pltpu.make_async_copy(attr_v.at[g], attr_out.at[:, g], attr_sem).start()
         for d in far_x:
-            j = (x + d) % nx
-            part = jnp.dot(attr, enc_v[j], preferred_element_type=jnp.float32)
-            pbuf[g, d - 1] = part.astype(jnp.bfloat16)
-            remote(
-                pbuf.at[g, d - 1], rsx.at[g, d - 1], rsx_send, rsx_recv.at[g, d - 1], layer, x_peer(d)
-            ).start()
-        pown[g] = jnp.dot(attr, enc_v[x], preferred_element_type=jnp.float32)
+            part = jnp.dot(attr, enc_v[(x + d) % nx], preferred_element_type=jnp.float32)
+            pbuf[g, d - 1] = part.reshape(nz, tok, width).astype(jnp.bfloat16)
+        for d in far_z + [0]:
+            k = (z + d) % nz
+            for e in far_x:
+                remote(
+                    pbuf.at[g, e - 1, k], rsx.at[g, e - 1, k], rsx_send, rsx_recv.at[g, d], layer, x_peer(e)
+                ).start()
+        own = jnp.dot(attr, enc_v[x], preferred_element_type=jnp.float32)
+        pown[g] = own.reshape(nz, tok, width)
 
     def reduce_x(g):
-        total = pown[g]
-        for d in near_x:
-            settle(rsx.at[g, d - 1], rsx_recv.at[g, d - 1])
-            total = total + rsx[g, d - 1].astype(jnp.float32)
-        zsend[g] = total.reshape(nz, tok, width).astype(jnp.bfloat16)
-        for d in far_z:
-            remote(
-                zsend.at[g, (z + d) % nz], rsz.at[g, d - 1], rsz_send, rsz_recv.at[g], layer, z_peer(d)
-            ).start()
+        for d in far_z + [0]:
+            k = (z + d) % nz
+            settle(rsx.at[g, :, k], rsx_recv.at[g, d])
+            total = pown[g, k]
+            for e in near_x:
+                total = total + rsx[g, e - 1, k].astype(jnp.float32)
+            zsend[g, k] = total.astype(jnp.bfloat16)
+            if d:
+                remote(zsend.at[g, k], rsz.at[g, d - 1], rsz_send, rsz_recv.at[g], layer, z_peer(d)).start()
 
     def reduce_z(g):
         @pl.when(jnp.logical_not(is_top))
@@ -163,7 +168,7 @@
         @pl.when(layer > 0)
         def _():
             for d in far_z + [0]:
-                remote(hout.at[g], agbuf.at[g, x, z], agz_send, agz_recv.at[g], lower, z_peer(d)).start()
+                remote(hout.at[g], agbuf.at[g, x, z], agz_send, agz_recv.at[g, d], lower, z_peer(d)).start()
             remote(gnew.at[g], gin.at[g], gin_send, gin_recv.at[g], lower, feat).start()
 
         @pl.when(x != g)
@@ -174,23 +179,12 @@
         def _():
             pltpu.make_async_copy(gnew.at[g], coll.at[x], coll_recv).start()
 
-    @pl.loop(0, groups + 1)
+    @pl.loop(0, groups)
     def _(step):
-        @pl.when(step < groups)
-        def _():
-            forward(step)
-
-        @pl.when(step > 0)
-        def _():
-            reduce_x(step - 1)
-
-        @pl.when(step < groups)
-        def _():
-            attribute(step)
-
-        @pl.when(step > 0)
-        def _():
-            reduce_z(step - 1)
+        forward(step)
+        attribute(step)
+        reduce_x(step)
+        reduce_z(step)
 
     settle(coll, coll_recv)
     for j in range(nx):
@@ -246,9 +240,9 @@
             pltpu.VMEM((nx, tok, width), f32),
             pltpu.VMEM((nx, tok, width), f32),
             pltpu.VMEM((nx, nx, nz, tok, width), bf16),
-            pltpu.VMEM((nx, nx - 1, rows, width), bf16),
-            pltpu.VMEM((nx, rows, width), f32),
-            pltpu.VMEM((nx, nx - 1, rows, width), bf16),
+            pltpu.VMEM((nx, nx - 1, nz, tok, width), bf16),
+            pltpu.VMEM((nx, nz, tok, width), f32),
+            pltpu.VMEM((nx, nx - 1, nz, tok, width), bf16),
             pltpu.VMEM((nx, nz, tok, width), bf16),
             pltpu.VMEM((nx, nz - 1, tok, width), bf16),
             pltpu.VMEM((nx, tok, width), f32),
@@ -257,11 +251,11 @@
             dma,
             dma,
             dma,
-            dma((nx,)),
+            dma((nx, nz)),
             dma,
             dma((nx, nx - 1)),
             dma,
-            dma((nx, nx - 1)),
+            dma((nx, nz)),
             dma,
             dma((nx,)),
             dma,

time: 283 us -> 260 us (0.919)
  Pallas kernels: 279 us -> 256 us
    pallas_call x1, Pallas kernels: 279 us -> 256 us  [body(): pl.pallas_call(functools.partial(kernel, layers, nz, nx), out_shape=(jax....]
where the time goes in v2:
time: 260 us
  Pallas kernels  256 us (98%)
  local copies, waits for them, and re-layouts  3.25 us (1%)
    pallas_call x1, Pallas kernels, body(): pl.pallas_call(functools.partial(kernel, layers, nz, nx), out_shape=(jax....  256 us

profile of v2, /device:TPU:6, one launch (start us, length us, event | category | flops | bytes accessed | tf_op | source)
XLA Modules:
  0.0 259.6 jit_solution(13067527463682946784)
XLA Ops:
  0.6 255.7 %shard_map.77 = (bf16[8,4,8,512]{3,2,1,0:T(8,128)(2,1)}, f32[8,4608]{1,0:T(8,128)}) custom-call(bf16[8,4608]{1,0:T(8,128)(2,1)} %top_ref.1, bf16[512,4608]{1,0:T(8,128)(2,1)} %bitcast.6, bf16[512,4608]{1,0:T(8,128)(2,1)} %bitcast.7, bf16[8,4,8,512]{3,2,1,0:T(8,128)(2,1)} %bitcast.8, s32[32,64]{1,0:T(8,128)} %bitcast.11, s32[1,32]{1,0:T(1,128)} %cnt_ref.1), custom_call_target="tpu_custom_call" | custom-call | tf_op jit(solution)/shard_map/pallas_call | solution.py:224
  256.3 1.7 copy.10
  258.0 1.6 copy.11

commit v3 on v2

--- a/solution.py
+++ b/solution.py
@@ -10,13 +10,20 @@
 BLOCK = 128
 MESH = pl.DeviceIdType.MESH
 NX = 4
+NEAR_IN = 2
+NEAR_OUT = 2
+
+
+def side_columns(nz, reach):
+    near = [d for d in sorted(range(nz), key=lambda d: min(d, nz - d)) if min(d, nz - d) <= reach]
+    return {d: 1 - 2 * (i % 2) for i, d in enumerate(near)}
 
 
 def kernel(
     layers, nz, nx, top_ref, dec_hbm, enc_hbm, act_hbm, ids_ref, cnt_ref, attr_out, grad_out,
-    dec_v, enc_v, act_v, gate_v, attr_v, hsend, hout, gin, gnew, agbuf, pbuf, pown, rsx, zsend, rsz, coll,
+    dec_v, enc_v, act_v, gate_v, attr_v, hsend, hout, gin, gnew, agbuf, pbuf, pown, rsx, zsend, zside, rsz, coll,
     load_sem, attr_sem, top_send, top_recv, agz_send, agz_recv, agx_send, agx_recv, rsx_send, rsx_recv,
-    rsz_send, rsz_recv, gin_send, gin_recv, coll_send, coll_recv,
+    rsz_send, rsz_recv, gin_send, gin_recv, coll_send, coll_recv, side_recv, agzs_send, agq_send, rsq_send, zside_send,
 ):
     feats, width = dec_v.shape[1], dec_v.shape[2]
     tok = top_ref.shape[0]
@@ -36,6 +43,9 @@
     def x_peer(d):
         return z * nx + (x + d) % nx
 
+    def corner(d, e):
+        return ((z + d) % nz) * nx + (x + e) % nx
+
     def cols(j):
         return pl.ds(pl.multiple_of(j * width, 128), width)
 
@@ -53,17 +63,22 @@
     for load in loads:
         load.start()
 
+    near_z = sorted(range(nz), key=lambda d: min(d, nz - d))
+    far_z = [d for d in near_z[::-1] if d]
+    sides = side_columns(nz, NEAR_IN)
+    backs = side_columns(nz, NEAR_OUT)
+
+    moves = [(0, 0, e) for e in range(1, nx)] + [(0, d, 0) for d in range(1, nz)]
+    moves += [(0, d, e) for d in {**sides, **backs} if d for e in (1, -1)]
+    moves += [(-1, d, 0) for d in range(nz)] + [(-1, d, e) for d, e in sides.items()]
+    moves += [(-a, -b, -c) for a, b, c in moves]
+    moves = sorted({(a % layers, b % nz, c % nx) for a, b, c in moves})
     barrier = pltpu.get_barrier_semaphore()
-    for d in range(1, nx):
-        pl.semaphore_signal(barrier, inc=1, device_id=(layer, x_peer(d)), device_id_type=MESH)
-    for d in range(1, nz):
-        pl.semaphore_signal(barrier, inc=1, device_id=(layer, z_peer(d)), device_id_type=MESH)
-    for d in range(nz):
-        pl.semaphore_signal(barrier, inc=1, device_id=(lower, z_peer(d)), device_id_type=MESH)
-        pl.semaphore_signal(barrier, inc=1, device_id=(upper, z_peer(d)), device_id_type=MESH)
-    pl.semaphore_wait(barrier, nx - 1 + nz - 1 + 2 * nz)
-
-    far_z = sorted(range(1, nz), key=lambda d: -min(d, nz - d))
+    for a, b, c in moves:
+        where = ((layer + a) % layers, ((z + b) % nz) * nx + (x + c) % nx)
+        pl.semaphore_signal(barrier, inc=1, device_id=where, device_id_type=MESH)
+    pl.semaphore_wait(barrier, len(moves))
+
     far_x = sorted(range(1, nx), key=lambda d: -min(d, nx - d))
     near_x = far_x[::-1]
 
@@ -81,6 +96,8 @@
             for d in far_z:
                 remote(hsend.at[g], agbuf.at[g, x, z], agz_send, agz_recv.at[g, d], layer, z_peer(d)).start()
             pltpu.make_async_copy(hsend.at[g], agbuf.at[g, x, z], agz_recv.at[g, 0]).start()
+            for d, e in sides.items():
+                remote(hsend.at[g], agbuf.at[g, x, z], agzs_send, side_recv.at[g, d], layer, corner(d, e)).start()
             gin[g] = hsend[g].astype(jnp.float32)
 
     tiles = nz * nx
@@ -106,48 +123,80 @@
     for load in loads[nx:]:
         load.wait()
 
+    def pass_on(g, j, k, send, e, d):
+        block = agbuf.at[g, j, k]
+        remote(block, block, send, agx_recv.at[g, e - 1], layer, x_peer(d)).start()
+
     def forward(g):
-        for d in [0] + far_z[::-1]:
+        for d in near_z:
             k = (z + nz - d) % nz
             settle(agbuf.at[g, x, k], agz_recv.at[g, d])
-            for e in far_x:
-                remote(
-                    agbuf.at[g, x, k], agbuf.at[g, x, k], agx_send, agx_recv.at[g, e - 1], layer, x_peer(e)
-                ).start()
+            if d in sides:
+                pass_on(g, x, k, agq_send, -sides[d] % nx, -sides[d])
+                j = (x + nx - sides[d]) % nx
+                settle(agbuf.at[g, j, k], side_recv.at[g, d])
+                pass_on(g, j, k, agq_send, 2, sides[d])
+            else:
+                for e in far_x:
+                    pass_on(g, x, k, agx_send, e, e)
 
     def scores_of(g, j):
         h = agbuf[g, j].reshape(rows, width)
         return lax.dot_general(h, dec_v[j], (((1,), (1,)), ((), ())), preferred_element_type=jnp.float32)
+
+    def out_x(g, d, e):
+        k = (z + d) % nz
+        remote(
+            pbuf.at[g, e - 1, k], rsx.at[g, e - 1, k], rsx_send, rsx_recv.at[g, d], layer, x_peer(e)
+        ).start()
 
     def attribute(g):
         total = scores_of(g, x)
         for d in near_x:
             j = (x + nx - d) % nx
-            settle(agbuf.at[g, j], agx_recv.at[g, d - 1])
+            passed = nz - sum(e % nx == d for e in sides.values())
+            settle(agbuf.at[g, j, pl.ds(0, passed)], agx_recv.at[g, d - 1])
             total = total + scores_of(g, j)
         attr = total * gate_v[g]
         attr_v[g] = attr.reshape(nz, tok, feats).astype(jnp.bfloat16)
         attr = attr.astype(jnp.bfloat16)
         pltpu.make_async_copy(attr_v.at[g], attr_out.at[:, g], attr_sem).start()
-        for d in far_x:
-            part = jnp.dot(attr, enc_v[(x + d) % nx], preferred_element_type=jnp.float32)
-            pbuf[g, d - 1] = part.reshape(nz, tok, width).astype(jnp.bfloat16)
+        plain = [d for d in far_z + [0] if d not in backs]
+        for e in far_x:
+            part = jnp.dot(attr, enc_v[(x + e) % nx], preferred_element_type=jnp.float32)
+            pbuf[g, e - 1] = part.reshape(nz, tok, width).astype(jnp.bfloat16)
+            for d in plain[:3]:
+                out_x(g, d, e)
         for d in far_z + [0]:
-            k = (z + d) % nz
-            for e in far_x:
+            if d in backs:
+                k, e = (z + d) % nz, backs[d]
+                remote(pbuf.at[g, 1, k], rsx.at[g, 1, k], rsq_send, rsx_recv.at[g, d], layer, x_peer(-e)).start()
                 remote(
-                    pbuf.at[g, e - 1, k], rsx.at[g, e - 1, k], rsx_send, rsx_recv.at[g, d], layer, x_peer(e)
+                    pbuf.at[g, e % nx - 1, k], rsx.at[g, 0, k], rsq_send, rsx_recv.at[g, d], layer, x_peer(e)
                 ).start()
+            elif d not in plain[:3]:
+                for e in far_x:
+                    out_x(g, d, e)
         own = jnp.dot(attr, enc_v[x], preferred_element_type=jnp.float32)
         pown[g] = own.reshape(nz, tok, width)
 
     def reduce_x(g):
         for d in far_z + [0]:
             k = (z + d) % nz
-            settle(rsx.at[g, :, k], rsx_recv.at[g, d])
             total = pown[g, k]
-            for e in near_x:
-                total = total + rsx[g, e - 1, k].astype(jnp.float32)
+            if d in backs:
+                e, i = backs[d], list(backs).index(d)
+                settle(rsx.at[g, pl.ds(0, 2), k], rsx_recv.at[g, d])
+                total = total + rsx[g, 0, k].astype(jnp.float32)
+                other = pbuf[g, -e % nx - 1, k].astype(jnp.float32) + rsx[g, 1, k].astype(jnp.float32)
+                zside[g, i] = other.astype(jnp.bfloat16)
+                remote(
+                    zside.at[g, i], rsz.at[g, nz - 1 + i], zside_send, rsz_recv.at[g], layer, corner(d, -e)
+                ).start()
+            else:
+                settle(rsx.at[g, :, k], rsx_recv.at[g, d])
+                for e in near_x:
+                    total = total + rsx[g, e - 1, k].astype(jnp.float32)
             zsend[g, k] = total.astype(jnp.bfloat16)
             if d:
                 remote(zsend.at[g, k], rsz.at[g, d - 1], rsz_send, rsz_recv.at[g], layer, z_peer(d)).start()
@@ -159,8 +208,8 @@
 
         settle(rsz.at[g], rsz_recv.at[g])
         total = zsend[g, z].astype(jnp.float32)
-        for d in range(1, nz):
-            total = total + rsz[g, d - 1].astype(jnp.float32)
+        for d in range(nz - 1 + len(backs)):
+            total = total + rsz[g, d].astype(jnp.float32)
         total = total + gin[g]
         gnew[g] = total
         hout[g] = total.astype(jnp.bfloat16)
@@ -169,6 +218,9 @@
         def _():
             for d in far_z + [0]:
                 remote(hout.at[g], agbuf.at[g, x, z], agz_send, agz_recv.at[g, d], lower, z_peer(d)).start()
+                if d in sides:
+                    where = corner(d, sides[d])
+                    remote(hout.at[g], agbuf.at[g, x, z], agzs_send, side_recv.at[g, d], lower, where).start()
             remote(gnew.at[g], gin.at[g], gin_send, gin_recv.at[g], lower, feat).start()
 
         @pl.when(x != g)
@@ -179,20 +231,35 @@
         def _():
             pltpu.make_async_copy(gnew.at[g], coll.at[x], coll_recv).start()
 
-    @pl.loop(0, groups)
+    @pl.loop(0, groups + 1)
     def _(step):
-        forward(step)
-        attribute(step)
-        reduce_x(step)
-        reduce_z(step)
+        @pl.when(step < groups)
+        def _():
+            forward(step)
+
+        @pl.when(step > 0)
+        def _():
+            reduce_z(step - 1)
+
+        @pl.when(step < groups)
+        def _():
+            attribute(step)
+            reduce_x(step)
 
     settle(coll, coll_recv)
     for j in range(nx):
         grad_out[:, j * width:(j + 1) * width] = coll[j]
 
     settle(attr_v, attr_sem)
-    settle(agbuf.at[:, pl.ds(0, nx - 1)], agx_send)
-    settle(pbuf, rsx_send)
+    for count, sem, small, ref in (
+        (len(sides), agx_send, agq_send, agbuf), (len(backs), rsx_send, rsq_send, pbuf)
+    ):
+        if count < nz:
+            settle(ref.at[:, pl.ds(0, nx - 1), pl.ds(0, nz - count)], sem)
+        if count:
+            settle(ref.at[:, pl.ds(0, 2), pl.ds(0, count)], small)
+    if backs:
+        settle(zside.at[:, pl.ds(0, len(backs))], zside_send)
     settle(zsend.at[:, pl.ds(0, nz - 1)], rsz_send)
     settle(coll.at[pl.ds(0, nx - 1)], coll_send)
 
@@ -200,10 +267,14 @@
     def _():
         settle(hsend.at[pl.ds(0, nx - 1)], top_send)
         settle(zsend.at[:, pl.ds(0, nz - 1)], agz_send)
+        if sides:
+            settle(zside.at[:, pl.ds(0, len(sides))], agzs_send)
 
     @pl.when(layer > 0)
     def _():
         settle(zsend, agz_send)
+        if sides:
+            settle(zside.at[:, pl.ds(0, len(sides))], agzs_send)
         settle(gnew, gin_send)
 
 
@@ -216,6 +287,8 @@
     width = model // nx
     tok = top_grad.shape[0]
     rows = nz * tok
+    extra = len(side_columns(nz, NEAR_OUT))
+    slots = max(1, extra, len(side_columns(nz, NEAR_IN)))
     act = activations[0].reshape(nz, nx, tok, feats)
     bf16, f32 = jnp.bfloat16, jnp.float32
     dma = pltpu.SemaphoreType.DMA
@@ -244,7 +317,8 @@
             pltpu.VMEM((nx, nz, tok, width), f32),
             pltpu.VMEM((nx, nx - 1, nz, tok, width), bf16),
             pltpu.VMEM((nx, nz, tok, width), bf16),
-            pltpu.VMEM((nx, nz - 1, tok, width), bf16),
+            pltpu.VMEM((nx, slots, tok, width), bf16),
+            pltpu.VMEM((nx, nz - 1 + extra, tok, width), bf16),
             pltpu.VMEM((nx, tok, width), f32),
             dma((3 * nx,)),
             dma,
@@ -260,6 +334,11 @@
             dma((nx,)),
             dma,
             dma((nx,)),
+            dma,
+            dma,
+            dma((nx, nz)),
+            dma,
+            dma,
             dma,
             dma,
         ],

time: 260 us -> 253 us (0.973)
  Pallas kernels: 256 us -> 249 us
    pallas_call x1, Pallas kernels: 256 us -> 249 us  [body(): pl.pallas_call(functools.partial(kernel, layers, nz, nx), out_shape=(jax....]
where the time goes in v3:
time: 253 us
  Pallas kernels  249 us (98%)
  local copies, waits for them, and re-layouts  3.25 us (1%)
    pallas_call x1, Pallas kernels, body(): pl.pallas_call(functools.partial(kernel, layers, nz, nx), out_shape=(jax....  249 us

profile of v3, /device:TPU:6, one launch (start us, length us, event | category | flops | bytes accessed | tf_op | source)
XLA Modules:
  0.0 252.9 jit_solution(8449276975385731272)
XLA Ops:
  0.6 249.0 %shard_map.77 = (bf16[8,4,8,512]{3,2,1,0:T(8,128)(2,1)}, f32[8,4608]{1,0:T(8,128)}) custom-call(bf16[8,4608]{1,0:T(8,128)(2,1)} %top_ref.1, bf16[512,4608]{1,0:T(8,128)(2,1)} %bitcast.6, bf16[512,4608]{1,0:T(8,128)(2,1)} %bitcast.7, bf16[8,4,8,512]{3,2,1,0:T(8,128)(2,1)} %bitcast.8, s32[32,64]{1,0:T(8,128)} %bitcast.11, s32[1,32]{1,0:T(1,128)} %cnt_ref.1), custom_call_target="tpu_custom_call" | custom-call | tf_op jit(solution)/shard_map/pallas_call | solution.py:297
  249.6 1.7 copy.10
  251.3 1.6 copy.11

commit v4 on v3

--- a/solution.py
+++ b/solution.py
@@ -127,15 +127,19 @@
         block = agbuf.at[g, j, k]
         remote(block, block, send, agx_recv.at[g, e - 1], layer, x_peer(d)).start()
 
+    arrivals = [(min(d, nz - d), 0, d) for d in near_z] + [(min(d, nz - d) + 1, 1, d) for d in sides]
+
     def forward(g):
-        for d in near_z:
+        for hops, second, d in sorted(arrivals):
             k = (z + nz - d) % nz
+            if second:
+                j = (x + nx - sides[d]) % nx
+                settle(agbuf.at[g, j, k], side_recv.at[g, d])
+                pass_on(g, j, k, agq_send, 2, sides[d])
+                continue
             settle(agbuf.at[g, x, k], agz_recv.at[g, d])
             if d in sides:
                 pass_on(g, x, k, agq_send, -sides[d] % nx, -sides[d])
-                j = (x + nx - sides[d]) % nx
-                settle(agbuf.at[g, j, k], side_recv.at[g, d])
-                pass_on(g, j, k, agq_send, 2, sides[d])
             else:
                 for e in far_x:
                     pass_on(g, x, k, agx_send, e, e)
@@ -276,6 +280,11 @@
         if sides:
             settle(zside.at[:, pl.ds(0, len(sides))], agzs_send)
         settle(gnew, gin_send)
+
+
+def hand_over(attr_ref, grad_ref, attr_out, grad_out):
+    attr_out[...] = attr_ref[...]
+    grad_out[...] = grad_ref[...]
 
 
 def body(nx, top_grad, decoder, encoder, activations, block_ids, block_counts):
@@ -346,6 +355,15 @@
             collective_id=0, has_side_effects=True, vmem_limit_bytes=60 * 1024 * 1024
         ),
     )(top_grad, dec, enc, act, block_ids[0], block_counts)
+    attr, grads = pl.pallas_call(
+        hand_over,
+        out_shape=(
+            jax.ShapeDtypeStruct((nz, nx, tok, feats), bf16),
+            jax.ShapeDtypeStruct((tok, model), f32),
+        ),
+        in_specs=[vmem, vmem],
+        out_specs=(vmem, vmem),
+    )(attr, grads)
     return (attr.reshape(1, tiles * tok, feats), grads[None])
 
 

time: 253 us -> 250 us (0.988)
  local copies, waits for them, and re-layouts: 3.25 us -> 0 us
    unnamed x2 -> x0, local copies, waits for them, and re-layouts: 3.25 us -> none
where the time goes in v4:
time: 250 us
  Pallas kernels  250 us (100%)
    pallas_call x1, Pallas kernels, body(): pl.pallas_call(functools.partial(kernel, layers, nz, nx), out_shape=(jax....  248 us

profile of v4, /device:TPU:6, one launch (start us, length us, event | category | flops | bytes accessed | tf_op | source)
XLA Modules:
  0.0 250.2 jit_solution(6896895613786093505)
XLA Ops:
  0.6 247.8 %shard_map.77 = (bf16[8,4,8,512]{3,2,1,0:T(8,128)(2,1)}, f32[8,4608]{1,0:T(8,128)}) custom-call(bf16[8,4608]{1,0:T(8,128)(2,1)} %top_ref.1, bf16[512,4608]{1,0:T(8,128)(2,1)} %bitcast.6, bf16[512,4608]{1,0:T(8,128)(2,1)} %bitcast.7, bf16[8,4,8,512]{3,2,1,0:T(8,128)(2,1)} %bitcast.8, s32[32,64]{1,0:T(8,128)} %bitcast.9, s32[1,32]{1,0:T(1,128)} %cnt_ref.1), custom_call_target="tpu_custom_call" | custom-call | tf_op jit(solution)/shard_map/pallas_call | solution.py:306
  248.4 1.8 shard_map.78

commit v5 on v4

--- a/solution.py
+++ b/solution.py
@@ -21,7 +21,7 @@
 
 def kernel(
     layers, nz, nx, top_ref, dec_hbm, enc_hbm, act_hbm, ids_ref, cnt_ref, attr_out, grad_out,
-    dec_v, enc_v, act_v, gate_v, attr_v, hsend, hout, gin, gnew, agbuf, pbuf, pown, rsx, zsend, zside, rsz, coll,
+    dec_v, enc_v, act_v, gate_v, attr_v, hsend, hout, gin, gnew, agbuf, pbuf, pown, rsx, zsend, zside, rsz, coll, begun,
     load_sem, attr_sem, top_send, top_recv, agz_send, agz_recv, agx_send, agx_recv, rsx_send, rsx_recv,
     rsz_send, rsz_recv, gin_send, gin_recv, coll_send, coll_recv, side_recv, agzs_send, agq_send, rsq_send, zside_send,
 ):
@@ -155,7 +155,7 @@
         ).start()
 
     def attribute(g):
-        total = scores_of(g, x)
+        total = begun[...]
         for d in near_x:
             j = (x + nx - d) % nx
             passed = nz - sum(e % nx == d for e in sides.values())
@@ -240,6 +240,7 @@
         @pl.when(step < groups)
         def _():
             forward(step)
+            begun[...] = scores_of(step, x)
 
         @pl.when(step > 0)
         def _():
@@ -329,6 +330,7 @@
             pltpu.VMEM((nx, slots, tok, width), bf16),
             pltpu.VMEM((nx, nz - 1 + extra, tok, width), bf16),
             pltpu.VMEM((nx, tok, width), f32),
+            pltpu.VMEM((rows, feats), f32),
             dma((3 * nx,)),
             dma,
             dma,

time: 250 us -> 249 us (level)
  no operation moved by 1% of the time
where the time goes in v5:
time: 249 us
  Pallas kernels  248 us (100%)
    pallas_call x1, Pallas kernels, body(): pl.pallas_call(functools.partial(kernel, layers, nz, nx), out_shape=(jax....  246 us

profile of v5, /device:TPU:6, one launch (start us, length us, event | category | flops | bytes accessed | tf_op | source)
XLA Modules:
  0.0 248.8 jit_solution(4853577020129003688)
XLA Ops:
  0.6 246.4 %shard_map.77 = (bf16[8,4,8,512]{3,2,1,0:T(8,128)(2,1)}, f32[8,4608]{1,0:T(8,128)}) custom-call(bf16[8,4608]{1,0:T(8,128)(2,1)} %top_ref.1, bf16[512,4608]{1,0:T(8,128)(2,1)} %bitcast.6, bf16[512,4608]{1,0:T(8,128)(2,1)} %bitcast.7, bf16[8,4,8,512]{3,2,1,0:T(8,128)(2,1)} %bitcast.8, s32[32,64]{1,0:T(8,128)} %bitcast.9, s32[1,32]{1,0:T(1,128)} %cnt_ref.1), custom_call_target="tpu_custom_call" | custom-call | tf_op jit(solution)/shard_map/pallas_call | solution.py:307
  247.0 1.8 shard_map.78
